TPU v7x, 32 devices: a whole 2x2x4 slice. The times are simulated.
32 devices in a mesh: frames: 16 (over z, y, core), dp: 2 (over x).
Axes of the slice: x: 2, y: 2, z: 4, core: 2. Of those that a mesh axis runs over, the one named last changes fastest.
Arguments:
- shifted: bfloat16 [2, 64, 16, 16, 640], P('dp', 'frames'), may hold values from -6 to 6
- out_grad: bfloat16 [2, 64, 16, 16, 640], P('dp', 'frames'), may hold values from -6 to 6
- conv_weight: bfloat16 [640, 5760], P('frames'), may hold values from -0.078125 to 0.078125
- norm_gain: float32 [640], replicated, may hold values from 0.5 to 2
- norm_bias: float32 [640], replicated, may hold values from -4 to 4
- shift_fwd: int32 [80], replicated, may hold values from 0 to 639, as said below
- shift_bwd: int32 [80], replicated, may hold values from 0 to 639, as said below
Outputs:
- in_grad: bfloat16 [2, 64, 16, 16, 640], P('dp', 'frames')
- weight_grad: float32 [640, 5760], P('frames')
- gain_grad: float32 [640], replicated
- bias_grad: float32 [640], replicated
Inputs may be any that keep to these rules, and one draw needn't show every extreme that they name: `shift_fwd`: 80 distinct channel numbers, none of them in shift_bwd. `shift_bwd`: 80 distinct channel numbers, none of them in shift_fwd.
All inputs are finite; a program needn't handle non-finite values.
Results may differ from a plain program's by a relative error of at most 0.003.
Values may be sent and summed in bfloat16 or wider, within the bound.
No kernel may reach another device: no remote copies, remote signals or barrier semaphores. Data moves between devices by JAX's collectives and lax.ppermute only.
A program may use at most 128 MiB of HBM per device.

v0:
```python
import jax
import jax.numpy as jnp
from jax import lax
from jax.sharding import PartitionSpec as P

GROUP_CH = 20
epsilon = 1e-05


def with_halo(x, sides, width):
    for axis, dim in sides:
        size, length = (lax.axis_size(axis), x.shape[dim])
        up = [(i, (i + 1) % size) for i in range(size - 1)]
        down = [(j, i) for i, j in up]
        last = lax.slice_in_dim(x, length - width, length, axis=dim)
        first = lax.slice_in_dim(x, 0, width, axis=dim)
        before = lax.ppermute(last, axis, up)
        after = lax.ppermute(first, axis, down)
        x = jnp.concatenate([before, x, after], axis=dim)
    return x


def pad_space(values):
    return jnp.pad(values, ((0, 0), (1, 1), (1, 1), (0, 0)))


def on_device(shifted, out_grad, conv_weight, norm_gain, norm_bias, shift_fwd, shift_bwd):
    frames_local = shifted[0]
    grad_local = out_grad[0]
    frame_count, row_count, col_count, channels = frames_local.shape
    groups = channels // GROUP_CH
    whole_weight = lax.all_gather(conv_weight, "frames", axis=0, tiled=True)
    values = frames_local.astype(jnp.float32).reshape(
        frame_count, row_count * col_count, groups, GROUP_CH
    )
    center = jnp.mean(values, axis=(1, 3), keepdims=True)
    spread = jnp.mean(jnp.square(values - center), axis=(1, 3), keepdims=True)
    inverse = lax.rsqrt(spread + epsilon)
    grouped_normed = (values - center) * inverse
    normed = grouped_normed.reshape(frame_count, row_count, col_count, channels)
    before = normed * norm_gain + norm_bias
    activation = jax.nn.silu(before).astype(jnp.bfloat16)
    act_padded = pad_space(activation)
    grad_padded = pad_space(grad_local)
    grad_rows = grad_local.reshape(-1, channels)
    act_grad = jnp.zeros((grad_rows.shape[0], channels), jnp.float32)
    for tap_index in range(9):
        row_off, col_off = divmod(tap_index, 3)
        grad_view = grad_padded[
            :, 2 - row_off : 2 - row_off + row_count, 2 - col_off : 2 - col_off + col_count, :
        ].reshape(-1, channels)
        act_grad = act_grad + jnp.dot(
            grad_view,
            whole_weight[:, tap_index * channels : (tap_index + 1) * channels],
            preferred_element_type=jnp.float32,
        )
    scale = float(
        lax.axis_size("dp") * lax.axis_size("frames") * frame_count * row_count * col_count
    ) ** (-0.5)
    parts = []
    for tap_index in range(9):
        row_off, col_off = divmod(tap_index, 3)
        act_view = act_padded[
            :, row_off : row_off + row_count, col_off : col_off + col_count, :
        ].reshape(-1, channels)
        parts.append(
            lax.dot_general(
                grad_rows, act_view, (((0,), (0,)), ((), ())), preferred_element_type=jnp.float32
            )
        )
    kernel_piece = lax.psum_scatter(
        jnp.concatenate(parts, axis=1), ("frames", "dp"), scatter_dimension=0, tiled=True
    )
    kernel_shard = lax.all_gather(kernel_piece, "dp", axis=0, tiled=True)
    weight_grad = kernel_shard * scale
    sigmoid_val = jax.nn.sigmoid(before)
    pre_grad = act_grad.reshape(before.shape) * sigmoid_val * (1.0 + before * (1.0 - sigmoid_val))
    gain_part = jnp.sum(pre_grad * normed, axis=(0, 1, 2))
    bias_part = jnp.sum(pre_grad, axis=(0, 1, 2))
    gain_total, bias_total = lax.psum((gain_part, bias_part), ("frames", "dp"))
    norm_grad = (pre_grad * norm_gain).reshape(values.shape)
    first_mean = jnp.mean(norm_grad, axis=(1, 3), keepdims=True)
    second_mean = jnp.mean(norm_grad * grouped_normed, axis=(1, 3), keepdims=True)
    shifted_grad = (
        ((norm_grad - first_mean - grouped_normed * second_mean) * inverse)
        .reshape(frames_local.shape)
        .astype(jnp.bfloat16)
    )
    channel_ids = jnp.arange(channels, dtype=jnp.int32)
    forward_match = channel_ids[None, :] == shift_fwd[:, None]
    backward_match = channel_ids[None, :] == shift_bwd[:, None]
    forward_select = forward_match.astype(jnp.bfloat16)
    backward_select = backward_match.astype(jnp.bfloat16)
    forward_mask = jnp.any(forward_match, axis=0)
    backward_mask = jnp.any(backward_match, axis=0)
    plane = row_count * col_count
    first_frame = shifted_grad[0].reshape(plane, channels)
    last_frame = shifted_grad[frame_count - 1].reshape(plane, channels)
    contract_channels = (((1,), (1,)), ((), ()))
    rim_first = lax.dot_general(
        forward_select, first_frame, contract_channels, preferred_element_type=jnp.float32
    ).astype(jnp.bfloat16)
    rim_last = lax.dot_general(
        backward_select, last_frame, contract_channels, preferred_element_type=jnp.float32
    ).astype(jnp.bfloat16)
    extended = with_halo(jnp.stack([rim_first, rim_last]), (("frames", 0),), 1)
    contract_fold = (((0,), (0,)), ((), ()))
    from_prev = lax.dot_general(
        extended[0], backward_select, contract_fold, preferred_element_type=jnp.float32
    ).astype(jnp.bfloat16)
    from_next = lax.dot_general(
        extended[3], forward_select, contract_fold, preferred_element_type=jnp.float32
    ).astype(jnp.bfloat16)
    from_prev = from_prev.reshape(1, row_count, col_count, channels)
    from_next = from_next.reshape(1, row_count, col_count, channels)
    later = jnp.concatenate([shifted_grad[1:], from_next], axis=0)
    earlier = jnp.concatenate([from_prev, shifted_grad[:-1]], axis=0)
    in_grad = jnp.where(forward_mask, later, jnp.where(backward_mask, earlier, shifted_grad))
    return (in_grad[None], weight_grad, gain_total * scale, bias_total * scale)


def solution(mesh):
    in_specs = (
        P("dp", "frames", None, None, None),
        P("dp", "frames", None, None, None),
        P("frames", None),
        P(),
        P(),
        P(),
        P(),
    )
    out_specs = (P("dp", "frames", None, None, None), P("frames", None), P(), P())
    return jax.shard_map(
        on_device, mesh=mesh, in_specs=in_specs, out_specs=out_specs, check_vma=False
    )
```

profile of v0, /device:TPU:0, one launch (start us, length us, event | category | flops | bytes accessed | tf_op | source)
XLA Modules:
  0.0 428.5 jit_solution(4472811872331687543)
XLA Ops:
  7.2 0.7 all-gather.3.cloned.1.call-update
  8.0 21.9 %reshape.226 = f32[4,256,32,20]{3,2,1,0:T(8,128)} reshape(bf16[1,4,16,16,640]{4,3,2,1,0:T(8,128)(2,1)} %param.7) | data formatting | bytes 3932160 | tf_op jit(solution)/shard_map/convert_element_type | solution.py:33
  29.9 0.2 convert_reduce_fusion
  30.1 0.1 reduce_sum.69
  30.2 0.1 reduce_sum.70
  30.3 0.1 copy.31
  30.5 0.1 sub.85
  30.6 0.4 multiply_reduce_fusion.2
  31.0 0.1 reduce_sum.72
  31.1 0.1 reduce_sum.73
  31.2 0.1 copy.33
  31.3 0.1 mul.189
  31.4 0.1 mul.190
  31.5 11.4 %copy.32 = f32[4,256,32,20]{1,0,3,2:T(4,128)} copy(f32[4,256,32,20]{3,2,1,0:T(8,128)} %reshape.226) | data formatting | bytes 5242880 | tf_op jit(solution)/shard_map/convert_element_type | solution.py:33
  42.9 0.1 add.132
  43.0 0.1 mul.201
  43.1 8.4 %pad_slice_fusion.8 = (bf16[4,16,16,640]{3,2,1,0:T(8,128)(2,1)S(1)}, bf16[4,16,16,640]{3,2,1,0:T(8,128)(2,1)}, bf16[4,16,16,640]{3,2,1,0:T(8,128)(2,1)}, bf16[4,...) fusion(bf16[4,16,16,640]{3,2,1,0:T(8,128)(2,1)} %bitcast.130), kind=kLoop, calls=%fused_computation.8 | loop fusion | bytes 11796480 | tf_op jit(solution)/shard_map/slice | solution.py:49
  51.5 29.3 %all-gather.3.cloned.1.call-done = bf16[640,5760]{1,0:T(8,128)(2,1)} async-done(((bf16[40,5760]{1,0:T(8,128)(2,1)}), bf16[640,5760]{1,0:T(8,128)(2,1)}) %all-gather.3.cloned.1.call-update) | async-done | bytes 7372816 | tf_op jit(solution)/shard_map/all_gather | solution.py:32
  80.8 3.0 fusion.4
  83.8 1.1 copy-done.10
  84.9 1.3 fusion.6
  86.3 1.3 fusion.8
  87.6 1.3 fusion.10
  89.0 1.3 fusion.12
  90.3 1.3 fusion.14
  91.7 1.3 fusion.18
  93.0 1.3 fusion.16
  94.3 5.4 %fusion.28 = (f32[640]{0:T(1024)S(1)}, f32[640]{0:T(1024)S(1)}, f32[1024,640]{1,0:T(8,128)}) fusion(f32[4,640]{1,0:T(4,128)S(1)} %mul.190, f32[4,640]{1,0:T(4,128)S(1)} %sub.85, bf16[1,4,16,16,640]{4,3,2,1,0:T(8,128)(2,1)S(1)} %copy-done, f32[640]{0:T(1024)S(1)} %copy-done.11, f32[640]{0:T(1024)S(1)} %copy-done.12, bf16[1024,640]{1,0:T(8,128)(2,1)S(1)} %bitcast.124, ...), kind=kOutput, calls=%fused_computation.87 | convolution fusion | flops 854588160 | bytes 27064320 | tf_op jit(solution)/shard_map/dot_general | solution.py:52
  99.7 3.2 copy.30
  103.0 4.2 reshape.215
  107.1 5.7 %fusion.29 = (f32[4,32]{0,1:T(8,128)S(1)}, f32[4,32]{0,1:T(8,128)S(1)}) fusion(f32[4,32]{0,1:T(8,128)S(1)} %copy.33, f32[4,256,32,20]{1,0,3,2:T(4,128)} %copy.32, f32[4,32]{0,1:T(8,128)S(1)} %copy.31, f32[4,256,32,20]{1,0,3,2:T(4,128)} %reshape.215, f32[32,20]{1,0:T(8,128)S(1)} %add.132, f32[32,20]{1,0:T(8,128)S(1)} %mul.201), kind=kLoop, calls=%fused_computation.88 | loop fusion | flops 10485504 | bytes 5250048 | tf_op jit(solution)/shard_map/reduce_sum | solution.py:82
  112.8 0.1 copy.35
  113.0 0.1 mul.210
  113.3 0.1 sub.95
  113.4 3.6 multiply_convert_fusion
  117.0 3.0 pad_slice_fusion
  120.0 2.4 bitcast_dynamic-update-slice_fusion.8
  122.4 2.4 bitcast_dynamic-update-slice_fusion.7
  124.8 2.4 bitcast_dynamic-update-slice_fusion.6
  127.3 2.4 bitcast_dynamic-update-slice_fusion.5
  129.7 2.4 bitcast_dynamic-update-slice_fusion.4
  132.1 2.4 bitcast_dynamic-update-slice_fusion.3
  134.5 2.5 bitcast_dynamic-update-slice_fusion.2
  137.0 2.4 bitcast_dynamic-update-slice_fusion.1
  139.4 2.4 bitcast_dynamic-update-slice_fusion
  141.9 0.6 copy-done.13
  142.5 0.1 fusion.20
  142.7 0.2 fusion.1
  143.0 1.3 collective-permute-start
  144.3 0.2 fusion.2
  144.5 3.0 collective-permute-start.1
  147.6 42.4 %all-reduce.3 = (f32[640]{0:T(1024)S(1)}, f32[640]{0:T(1024)S(1)}) all-reduce(f32[640]{0:T(1024)S(1)} %get-tuple-element.5, f32[640]{0:T(1024)S(1)} %get-tuple-element.4), channel_id=1, replica_groups=mesh['frames'=16,'dp'=2] {'frames','dp'}, use_global_device_ids=true, to_apply=%region_10.11 | all-reduce | flops 1280 | bytes 10240 | tf_op jit(solution)/shard_map/psum | solution.py:80
  189.9 0.2 slice_bitcast_fusion
  190.1 0.6 broadcast_multiply_fusion.1
  190.7 0.3 convolution_convert_fusion.1
  191.0 0.3 convolution_convert_fusion
  191.3 0.4 copy-done.1
  191.8 3.0 maximum_select_fusion
  194.7 203.1 %all-reduce.6.cloned.1.call-done = f32[640,5760]{0,1:T(8,128)} async-done(((f32[640,5760]{0,1:T(8,128)}), f32[640,5760]{0,1:T(8,128)}) %all-reduce.6.cloned.1.call-update) | async-done | bytes 14745616
  397.9 5.1 %dynamic-slice_bitcast_fusion = f32[1,20,5760]{1,2,0:T(8,128)} fusion(f32[640,5760]{0,1:T(8,128)} %all-reduce.6.cloned.1.call-done, u32[]{:T(128)S(6)} %multiply.25), kind=kLoop, calls=%fused_computation.16 | loop fusion | bytes 921604
  402.9 2.6 copy.36
  405.5 15.0 %all-gather = f32[2,20,5760]{2,1,0:T(8,128)S(1)} all-gather(f32[1,20,5760]{2,1,0:T(8,128)S(1)} %copy.36), channel_id=1, replica_groups=mesh['frames'=16,'dp'=2] {'dp'}, dimensions={0}, use_global_device_ids=true | all-gather | bytes 1382400 | tf_op jit(solution)/shard_map/all_gather | solution.py:74
  420.5 0.1 broadcast_multiply_fusion
  420.6 1.0 reshape.231
  (41 shorter events, 0.6 us)
Async XLA Ops:
  7.2 73.6 %all-gather.3.cloned.1.call-start = ((), (), s32[]{:S(2)}) async-start(), calls=%async_computation | async-start | bytes 7833600 | tf_op jit(solution)/shard_map/all_gather | solution.py:32
  7.9 22.0 %copy-start = (bf16[1,4,16,16,640]{4,3,2,1,0:T(8,128)(2,1)S(1)}, bf16[1,4,16,16,640]{4,3,2,1,0:T(8,128)(2,1)}, u32[]{:S(2)}) copy-start(bf16[1,4,16,16,640]{4,3,2,1,0:T(8,128)(2,1)} %param.7) | copy-start | bytes 3932164
  7.9 389.9 %all-reduce.6.cloned.1.call-start = ((), (), s32[]{:S(2)}) async-start(), calls=%async_computation.1 | async-start | bytes 29491200
  31.5 11.4 %copy-start.11 = (f32[640]{0:T(1024)S(1)}, f32[640]{0:T(1024)}, u32[]{:S(2)}) copy-start(f32[640]{0:T(1024)} %param.11) | copy-start | bytes 7684
  31.5 11.5 %copy-start.12 = (f32[640]{0:T(1024)S(1)}, f32[640]{0:T(1024)}, u32[]{:S(2)}) copy-start(f32[640]{0:T(1024)} %param.10) | copy-start | bytes 7684
  80.8 3.0 copy-start.9
  80.8 4.1 copy-start.10
  84.9 1.3 copy-start.8
  86.2 1.3 copy-start.2
  87.6 1.3 copy-start.7
  88.9 1.3 copy-start.6
  90.3 1.3 copy-start.5
  91.6 1.3 copy-start.4
  117.0 3.0 copy-start.3
  141.9 0.7 copy-start.13
  141.9 0.7 copy-start.14
  143.0 47.7 %collective-permute-start = (bf16[1,80,256]{2,1,0:T(8,128)(2,1)S(1)}, bf16[1,80,256]{2,1,0:T(8,128)(2,1)S(1)}, u32[]{:S(2)}, u32[]{:S(2)}) collective-permute-start(bf16[1,80,256]{2,1,0:T(8,128)(2,1)S(1)} %fusion.1), channel_id=1, source_target_pairs={{2,0},{4,2},{6,4},{8,6},{10,8},{12,10},{14,12},{16,14},{18,16},{20... | collective-permute-start | bytes 122888 | tf_op jit(solution)/shard_map/ppermute | solution.py:18
  144.5 46.5 %collective-permute-start.1 = (bf16[1,80,256]{2,1,0:T(8,128)(2,1)S(1)}, bf16[1,80,256]{2,1,0:T(8,128)(2,1)S(1)}, u32[]{:S(2)}, u32[]{:S(2)}) collective-permute-start(bf16[1,80,256]{2,1,0:T(8,128)(2,1)S(1)} %fusion.2), channel_id=1, source_target_pairs={{0,2},{2,4},{4,6},{6,8},{8,10},{10,12},{12,14},{14,16},{16,18},{18... | collective-permute-start | bytes 122888 | tf_op jit(solution)/shard_map/ppermute | solution.py:17
  189.9 1.8 copy-start.1
Sparse Core Ops, SparseCore 0:
  10.1 70.5 all-gather.2
  142.0 255.7 all-reduce.5
where the time goes:
time: 429 us; the launch traced here: 428 us
  waiting for transfers between devices  233 us (54%)
  local copies, waits for them, and re-layouts  64.8 us (15%)
  blocking collectives  57.4 us (13%)
  matrix products  40.6 us (9%)
  between operations  14.4 us (3%)
  other arithmetic  13.8 us (3%)
  starting transfers between devices  4.4 us (1%)
    unnamed x3, waiting for transfers between devices  204 us
    psum x1, blocking collectives, on_device(): gain_total, bias_total = lax.psum((gain_part, bias_part), ('frames', 'dp'))  42.4 us
    convert_element_type x2, local copies, waits for them, and re-layouts, on_device(): frames_local.astype(jnp.float32)  33.3 us
    all_gather x1, waiting for transfers between devices, on_device(): whole_weight = lax.all_gather(conv_weight, 'frames', axis=0, tiled=True)  29.3 us
    dot_general x9, matrix products, on_device(): lax.dot_general(grad_rows, act_view, (((0,), (0,)), ((), ())), preferred_...  21.8 us
    dot_general x9, matrix products, on_device(): jnp.dot(grad_view, whole_weight[:, tap_index * channels:(tap_index + 1) *...  17.7 us
    all_gather x1, blocking collectives, on_device(): kernel_shard = lax.all_gather(kernel_piece, 'dp', axis=0, tiled=True)  15 us
    unnamed x32, local copies, waits for them, and re-layouts  9.92 us
  transfers between devices with their start and end apart: 4, of which 2 were waited for; matrix products, arithmetic and copies ran while one was open for 11% of the time, Pallas kernels for 0%

commit v1 on v0

--- a/solution.py
+++ b/solution.py
@@ -5,6 +5,22 @@
 
 GROUP_CH = 20
 epsilon = 1e-05
+
+
+def ring_gather(x, axis, dim):
+    ways, here, step = (lax.axis_size(axis), lax.axis_index(axis), x.shape[dim])
+    shape = [n * ways if d == dim else n for d, n in enumerate(x.shape)]
+    full = lax.dynamic_update_slice_in_dim(jnp.zeros(shape, x.dtype), x, here * step, axis=dim)
+    going_up = going_down = x
+    for far in range(1, ways // 2 + 1):
+        going_up = lax.ppermute(going_up, axis, [(d, (d + 1) % ways) for d in range(ways)])
+        full = lax.dynamic_update_slice_in_dim(full, going_up, (here - far) % ways * step, axis=dim)
+        if 2 * far < ways:
+            going_down = lax.ppermute(going_down, axis, [(d, (d - 1) % ways) for d in range(ways)])
+            full = lax.dynamic_update_slice_in_dim(
+                full, going_down, (here + far) % ways * step, axis=dim
+            )
+    return full
 
 
 def with_halo(x, sides, width):
@@ -29,7 +45,7 @@
     grad_local = out_grad[0]
     frame_count, row_count, col_count, channels = frames_local.shape
     groups = channels // GROUP_CH
-    whole_weight = lax.all_gather(conv_weight, "frames", axis=0, tiled=True)
+    whole_weight = ring_gather(conv_weight, "frames", 0)
     values = frames_local.astype(jnp.float32).reshape(
         frame_count, row_count * col_count, groups, GROUP_CH
     )

time: 429 us -> 507 us (1.18); the launches traced: 428 us -> 500 us
  starting transfers between devices: 4.4 us -> 48.1 us
  local copies, waits for them, and re-layouts: 64.8 us -> 77.8 us
  matrix products: 40.6 us -> 48.5 us
    ppermute x0 -> x15, starting transfers between devices: none -> 41.8 us  [the longest x8 21.9 us: ring_gather(): lax.ppermute(going_up, axis, [(d, (d + 1) % ways) for d in range(ways)])]
    ppermute x0 -> x15, waiting for transfers between devices: none -> 30.4 us  [the longest x8 30.3 us: ring_gather(): lax.ppermute(going_up, axis, [(d, (d + 1) % ways) for d in range(ways)])]
    all_gather x1 -> x0, waiting for transfers between devices: 29.3 us -> none  [on_device(): whole_weight = lax.all_gather(conv_weight, 'frames', axis=0, tiled=True)]
    dynamic_update_slice x0 -> x16, local copies, waits for them, and re-layouts: none -> 14 us  [the longest x8 7.47 us: ring_gather(): lax.dynamic_update_slice_in_dim(full, going_up, (here - far) % ways * ste...]
    dot_general x9, matrix products: 17.7 us -> 25.6 us  [on_device(): jnp.dot(grad_view, whole_weight[:, tap_index * channels:(tap_index + 1) *...]
    slice x1, local copies, waits for them, and re-layouts: 8.36 us -> 3.14 us  [on_device(): grad_padded[:, 2 - row_off:2 - row_off + row_count, 2 - col_off:2 - col_o...]
    unnamed x3 -> x2, waiting for transfers between devices: 204 us -> 204 us
  transfers between devices with their start and end apart: 4 -> 18, of which waited for: 2 -> 8; matrix products, arithmetic and copies ran while one was open for 11% -> 13% of each run, Pallas kernels for 0% -> 0%
where the time goes in v1:
time: 507 us; the launch traced here: 500 us
  waiting for transfers between devices  235 us (46%)
  local copies, waits for them, and re-layouts  77.8 us (15%)
  blocking collectives  59.7 us (12%)
  matrix products  48.5 us (10%)
  starting transfers between devices  48.1 us (9%)
  other arithmetic  16.4 us (3%)
  between operations  14.6 us (3%)
    unnamed x2, waiting for transfers between devices  204 us
    psum x1, blocking collectives, on_device(): gain_total, bias_total = lax.psum((gain_part, bias_part), ('frames', 'dp'))  44.7 us
    convert_element_type x2, local copies, waits for them, and re-layouts, on_device(): frames_local.astype(jnp.float32)  32 us
    ppermute x8, waiting for transfers between devices, ring_gather(): lax.ppermute(going_up, axis, [(d, (d + 1) % ways) for d in range(ways)])  30.3 us
    dot_general x9, matrix products, on_device(): jnp.dot(grad_view, whole_weight[:, tap_index * channels:(tap_index + 1) *...  25.6 us
    ppermute x8, starting transfers between devices, ring_gather(): lax.ppermute(going_up, axis, [(d, (d + 1) % ways) for d in range(ways)])  21.9 us
    dot_general x9, matrix products, on_device(): lax.dot_general(grad_rows, act_view, (((0,), (0,)), ((), ())), preferred_...  21.8 us
    ppermute x7, starting transfers between devices, ring_gather(): lax.ppermute(going_down, axis, [(d, (d - 1) % ways) for d in range(ways)])  20 us
  transfers between devices with their start and end apart: 18, of which 8 were waited for; matrix products, arithmetic and copies ran while one was open for 13% of the time, Pallas kernels for 0%

profile of v1, /device:TPU:0, one launch (start us, length us, event | category | flops | bytes accessed | tf_op | source)
XLA Modules:
  0.0 500.0 jit_solution(9053143046980167805)
XLA Ops:
  7.8 5.0 %collective-permute-start.1 = (bf16[40,5760]{1,0:T(8,128)(2,1)}, bf16[40,5760]{1,0:T(8,128)(2,1)S(1)}, u32[]{:S(2)}, u32[]{:S(2)}) collective-permute-start(bf16[40,5760]{1,0:T(8,128)(2,1)} %param.9), channel_id=1, source_target_pairs={{0,30},{2,0},{4,2},{6,4},{8,6},{10,8},{12,10},{14,12},{16,14},{18,... | collective-permute-start | bytes 1382408 | tf_op jit(solution)/shard_map/ppermute | solution.py:19
  12.8 1.5 convert_reduce_fusion
  14.8 1.7 multiply_reduce_fusion.2
  16.7 3.4 broadcast_in_dim.9
  20.9 20.5 %reshape.226 = f32[4,256,32,20]{3,2,1,0:T(8,128)} reshape(bf16[1,4,16,16,640]{4,3,2,1,0:T(8,128)(2,1)S(1)} %copy-done) | data formatting | bytes 3932160 | tf_op jit(solution)/shard_map/convert_element_type | solution.py:49
  43.7 11.5 %copy.37 = f32[4,256,32,20]{1,0,3,2:T(4,128)} copy(f32[4,256,32,20]{3,2,1,0:T(8,128)} %reshape.226) | data formatting | bytes 5242880 | tf_op jit(solution)/shard_map/convert_element_type | solution.py:49
  56.5 3.1 pad_slice_fusion.8
  59.8 4.4 collective-permute-start.3
  64.2 1.8 constant_dynamic-update-slice_fusion.14
  66.8 3.9 collective-permute-done.2
  70.7 4.4 collective-permute-start.5
  75.1 0.8 constant_dynamic-update-slice_fusion.12
  76.0 0.8 constant_dynamic-update-slice_fusion.11
  76.8 4.6 collective-permute-done.4
  82.2 3.6 collective-permute-start.7
  85.9 0.8 constant_dynamic-update-slice_fusion.10
  86.7 0.8 constant_dynamic-update-slice_fusion.9
  87.5 4.6 collective-permute-done.6
  92.1 2.2 collective-permute-start.8
  94.3 2.3 collective-permute-start.9
  97.4 0.8 constant_dynamic-update-slice_fusion.7
  98.2 4.7 collective-permute-done.8
  102.9 4.3 collective-permute-start.10
  107.3 0.8 constant_dynamic-update-slice_fusion.6
  108.9 4.6 collective-permute-done.10
  113.6 6.5 %collective-permute-start.12 = (bf16[40,5760]{1,0:T(8,128)(2,1)S(1)}, bf16[40,5760]{1,0:T(8,128)(2,1)S(1)}, u32[]{:S(2)}, u32[]{:S(2)}) collective-permute-start(bf16[40,5760]{1,0:T(8,128)(2,1)S(1)} %collective-permute-done.10), channel_id=1, source_target_pairs={{0,2},{2,4},{4,6},{6,8},{8,10},{10,12},{12,14},{14,16},{16,18},{18... | collective-permute-start | bytes 1382408 | tf_op jit(solution)/shard_map/ppermute | solution.py:16
  120.0 0.8 constant_dynamic-update-slice_fusion.4
  120.9 0.8 constant_dynamic-update-slice_fusion.3
  121.7 3.9 collective-permute-done.12
  125.6 7.5 %collective-permute-start.14 = (bf16[40,5760]{1,0:T(8,128)(2,1)S(1)}, bf16[40,5760]{1,0:T(8,128)(2,1)S(1)}, u32[]{:S(2)}, u32[]{:S(2)}) collective-permute-start(bf16[40,5760]{1,0:T(8,128)(2,1)S(1)} %collective-permute-done.12), channel_id=1, source_target_pairs={{0,2},{2,4},{4,6},{6,8},{8,10},{10,12},{12,14},{14,16},{16,18},{18... | collective-permute-start | bytes 1382408 | tf_op jit(solution)/shard_map/ppermute | solution.py:16
  134.0 0.8 constant_dynamic-update-slice_fusion.1
  134.8 3.9 collective-permute-done.14
  139.5 2.5 fusion.11
  142.0 2.5 fusion.13
  144.5 2.5 fusion.15
  147.0 2.5 fusion.17
  149.4 2.5 fusion.19
  151.9 2.5 fusion.21
  154.4 2.5 fusion.25
  156.9 2.5 fusion.23
  159.4 5.9 %fusion.35 = (f32[640]{0:T(1024)S(1)}, f32[640]{0:T(1024)S(1)}, f32[1024,640]{1,0:T(8,128)}) fusion(f32[4,640]{1,0:T(4,128)S(1)} %copy-done.7, f32[4,640]{1,0:T(4,128)S(1)} %copy-done.6, bf16[1,4,16,16,640]{4,3,2,1,0:T(8,128)(2,1)S(1)} %copy-done, f32[640]{0:T(1024)S(1)} %copy-done.12, f32[640]{0:T(1024)S(1)} %copy-done.13, ...), kind=kOutput, calls=%fused_computation.108 | convolution fusion | flops 854588160 | bytes 27064320 | tf_op jit(solution)/shard_map/dot_general | solution.py:68
  165.3 3.2 copy.35
  168.5 4.2 reshape.215
  172.8 5.7 %fusion.36 = (f32[4,32]{0,1:T(8,128)S(1)}, f32[4,32]{0,1:T(8,128)S(1)}) fusion(f32[4,32]{0,1:T(8,128)S(1)} %copy-done.11, f32[4,256,32,20]{1,0,3,2:T(4,128)} %copy.37, f32[4,32]{0,1:T(8,128)S(1)} %copy-done.10, f32[4,256,32,20]{1,0,3,2:T(4,128)} %reshape.215, f32[32,20]{1,0:T(8,128)S(1)} %copy-done.8, f32[32,20]{1,0:T(8,128)S(1)} %copy-done.9), kind=kLoop, calls=%fused_computation.109 | loop fusion | flops 10485504 | bytes 5250048 | tf_op jit(solution)/shard_map/reduce_sum | solution.py:98
  179.0 3.6 multiply_convert_fusion
  182.6 3.2 pad_slice_fusion
  185.8 2.4 bitcast_dynamic-update-slice_fusion.8
  188.2 2.4 bitcast_dynamic-update-slice_fusion.7
  190.7 2.4 bitcast_dynamic-update-slice_fusion.6
  193.1 2.4 bitcast_dynamic-update-slice_fusion.5
  195.5 2.4 bitcast_dynamic-update-slice_fusion.4
  197.9 2.4 bitcast_dynamic-update-slice_fusion.3
  200.3 2.5 bitcast_dynamic-update-slice_fusion.2
  202.8 2.4 bitcast_dynamic-update-slice_fusion.1
  205.2 2.4 bitcast_dynamic-update-slice_fusion
  208.7 1.3 collective-permute-start.15
  210.3 4.9 collective-permute-start.16
  215.2 44.7 %all-reduce.3 = (f32[640]{0:T(1024)S(1)}, f32[640]{0:T(1024)S(1)}) all-reduce(f32[640]{0:T(1024)S(1)} %get-tuple-element.5, f32[640]{0:T(1024)S(1)} %get-tuple-element.4), channel_id=1, replica_groups=mesh['frames'=16,'dp'=2] {'frames','dp'}, use_global_device_ids=true, to_apply=%region_10.11 | all-reduce | flops 1280 | bytes 10240 | tf_op jit(solution)/shard_map/psum | solution.py:96
  261.7 3.0 maximum_select_fusion
  264.7 204.4 %all-reduce.6.cloned.1.call-done = f32[640,5760]{0,1:T(8,128)} async-done(((f32[640,5760]{0,1:T(8,128)}), f32[640,5760]{0,1:T(8,128)}) %all-reduce.6.cloned.1.call-update) | async-done | bytes 14745616
  469.1 5.1 %dynamic-slice_bitcast_fusion = f32[1,20,5760]{1,2,0:T(8,128)} fusion(f32[640,5760]{0,1:T(8,128)} %all-reduce.6.cloned.1.call-done, u32[]{:T(128)S(6)} %multiply.25), kind=kLoop, calls=%fused_computation.16 | loop fusion | bytes 921604
  474.2 2.6 copy.41
  476.8 15.0 %all-gather = f32[2,20,5760]{2,1,0:T(8,128)S(1)} all-gather(f32[1,20,5760]{2,1,0:T(8,128)S(1)} %copy.41), channel_id=1, replica_groups=mesh['frames'=16,'dp'=2] {'dp'}, dimensions={0}, use_global_device_ids=true | all-gather | bytes 1382400 | tf_op jit(solution)/shard_map/all_gather | solution.py:90
  491.9 1.0 reshape.231
  (87 shorter events, 14.4 us)
Async XLA Ops:
  7.2 461.9 %all-reduce.6.cloned.1.call-start = ((), (), s32[]{:S(2)}) async-start(), calls=%async_computation | async-start | bytes 29491200
  7.2 52.5 %collective-permute-start = (bf16[40,5760]{1,0:T(8,128)(2,1)}, bf16[40,5760]{1,0:T(8,128)(2,1)}, u32[]{:S(2)}, u32[]{:S(2)}) collective-permute-start(bf16[40,5760]{1,0:T(8,128)(2,1)} %param.9), channel_id=1, source_target_pairs={{0,2},{2,4},{4,6},{6,8},{8,10},{10,12},{12,14},{14,16},{16,18},{18... | collective-permute-start | bytes 1382408 | tf_op jit(solution)/shard_map/ppermute | solution.py:16
  7.8 52.0 %collective-permute-start.1 = (bf16[40,5760]{1,0:T(8,128)(2,1)}, bf16[40,5760]{1,0:T(8,128)(2,1)S(1)}, u32[]{:S(2)}, u32[]{:S(2)}) collective-permute-start(bf16[40,5760]{1,0:T(8,128)(2,1)} %param.9), channel_id=1, source_target_pairs={{0,30},{2,0},{4,2},{6,4},{8,6},{10,8},{12,10},{14,12},{16,14},{18,... | collective-permute-start | bytes 1382408 | tf_op jit(solution)/shard_map/ppermute | solution.py:19
  14.7 1.9 copy-start.5
  16.7 3.5 copy-start.4
  16.7 4.3 copy-start
  43.7 11.5 %copy-start.12 = (f32[640]{0:T(1024)S(1)}, f32[640]{0:T(1024)}, u32[]{:S(2)}) copy-start(f32[640]{0:T(1024)} %param.11) | copy-start | bytes 7684
  43.7 12.2 %copy-start.13 = (f32[640]{0:T(1024)S(1)}, f32[640]{0:T(1024)}, u32[]{:S(2)}) copy-start(f32[640]{0:T(1024)} %param.10) | copy-start | bytes 7684
  43.7 12.9 %copy-start.2 = (bf16[1,4,16,16,640]{4,3,2,1,0:T(8,128)(2,1)S(1)}, bf16[1,4,16,16,640]{4,3,2,1,0:T(8,128)(2,1)}, u32[]{:S(2)}) copy-start(bf16[1,4,16,16,640]{4,3,2,1,0:T(8,128)(2,1)} %param.8) | copy-start | bytes 3932164
  59.7 11.0 %collective-permute-start.2 = (bf16[40,5760]{1,0:T(8,128)(2,1)}, bf16[40,5760]{1,0:T(8,128)(2,1)S(1)}, u32[]{:S(2)}, u32[]{:S(2)}) collective-permute-start(bf16[40,5760]{1,0:T(8,128)(2,1)} %collective-permute-done), channel_id=1, source_target_pairs={{0,2},{2,4},{4,6},{6,8},{8,10},{10,12},{12,14},{14,16},{16,18},{18... | collective-permute-start | bytes 1382408 | tf_op jit(solution)/shard_map/ppermute | solution.py:16
  59.8 10.9 %collective-permute-start.3 = (bf16[40,5760]{1,0:T(8,128)(2,1)S(1)}, bf16[40,5760]{1,0:T(8,128)(2,1)S(1)}, u32[]{:S(2)}, u32[]{:S(2)}) collective-permute-start(bf16[40,5760]{1,0:T(8,128)(2,1)S(1)} %collective-permute-done.1), channel_id=1, source_target_pairs={{0,30},{2,0},{4,2},{6,4},{8,6},{10,8},{12,10},{14,12},{16,14},{18,... | collective-permute-start | bytes 1382408 | tf_op jit(solution)/shard_map/ppermute | solution.py:19
  70.7 10.7 %collective-permute-start.4 = (bf16[40,5760]{1,0:T(8,128)(2,1)S(1)}, bf16[40,5760]{1,0:T(8,128)(2,1)S(1)}, u32[]{:S(2)}, u32[]{:S(2)}) collective-permute-start(bf16[40,5760]{1,0:T(8,128)(2,1)S(1)} %collective-permute-done.2), channel_id=1, source_target_pairs={{0,2},{2,4},{4,6},{6,8},{8,10},{10,12},{12,14},{14,16},{16,18},{18... | collective-permute-start | bytes 1382408 | tf_op jit(solution)/shard_map/ppermute | solution.py:16
  70.7 11.5 %collective-permute-start.5 = (bf16[40,5760]{1,0:T(8,128)(2,1)S(1)}, bf16[40,5760]{1,0:T(8,128)(2,1)S(1)}, u32[]{:S(2)}, u32[]{:S(2)}) collective-permute-start(bf16[40,5760]{1,0:T(8,128)(2,1)S(1)} %collective-permute-done.3), channel_id=1, source_target_pairs={{0,30},{2,0},{4,2},{6,4},{8,6},{10,8},{12,10},{14,12},{16,14},{18,... | collective-permute-start | bytes 1382408 | tf_op jit(solution)/shard_map/ppermute | solution.py:19
  81.4 10.7 %collective-permute-start.6 = (bf16[40,5760]{1,0:T(8,128)(2,1)S(1)}, bf16[40,5760]{1,0:T(8,128)(2,1)S(1)}, u32[]{:S(2)}, u32[]{:S(2)}) collective-permute-start(bf16[40,5760]{1,0:T(8,128)(2,1)S(1)} %collective-permute-done.4), channel_id=1, source_target_pairs={{0,2},{2,4},{4,6},{6,8},{8,10},{10,12},{12,14},{14,16},{16,18},{18... | collective-permute-start | bytes 1382408 | tf_op jit(solution)/shard_map/ppermute | solution.py:16
  82.2 12.1 %collective-permute-start.7 = (bf16[40,5760]{1,0:T(8,128)(2,1)S(1)}, bf16[40,5760]{1,0:T(8,128)(2,1)S(1)}, u32[]{:S(2)}, u32[]{:S(2)}) collective-permute-start(bf16[40,5760]{1,0:T(8,128)(2,1)S(1)} %collective-permute-done.5), channel_id=1, source_target_pairs={{0,30},{2,0},{4,2},{6,4},{8,6},{10,8},{12,10},{14,12},{16,14},{18,... | collective-permute-start | bytes 1382408 | tf_op jit(solution)/shard_map/ppermute | solution.py:19
  92.1 10.7 %collective-permute-start.8 = (bf16[40,5760]{1,0:T(8,128)(2,1)S(1)}, bf16[40,5760]{1,0:T(8,128)(2,1)S(1)}, u32[]{:S(2)}, u32[]{:S(2)}) collective-permute-start(bf16[40,5760]{1,0:T(8,128)(2,1)S(1)} %collective-permute-done.6), channel_id=1, source_target_pairs={{0,2},{2,4},{4,6},{6,8},{8,10},{10,12},{12,14},{14,16},{16,18},{18... | collective-permute-start | bytes 1382408 | tf_op jit(solution)/shard_map/ppermute | solution.py:16
  94.3 12.9 %collective-permute-start.9 = (bf16[40,5760]{1,0:T(8,128)(2,1)S(1)}, bf16[40,5760]{1,0:T(8,128)(2,1)S(1)}, u32[]{:S(2)}, u32[]{:S(2)}) collective-permute-start(bf16[40,5760]{1,0:T(8,128)(2,1)S(1)} %collective-permute-done.7), channel_id=1, source_target_pairs={{0,30},{2,0},{4,2},{6,4},{8,6},{10,8},{12,10},{14,12},{16,14},{18,... | collective-permute-start | bytes 1382408 | tf_op jit(solution)/shard_map/ppermute | solution.py:19
  102.9 10.7 %collective-permute-start.10 = (bf16[40,5760]{1,0:T(8,128)(2,1)S(1)}, bf16[40,5760]{1,0:T(8,128)(2,1)S(1)}, u32[]{:S(2)}, u32[]{:S(2)}) collective-permute-start(bf16[40,5760]{1,0:T(8,128)(2,1)S(1)} %collective-permute-done.8), channel_id=1, source_target_pairs={{0,2},{2,4},{4,6},{6,8},{8,10},{10,12},{12,14},{14,16},{16,18},{18... | collective-permute-start | bytes 1382408 | tf_op jit(solution)/shard_map/ppermute | solution.py:16
  107.2 12.9 %collective-permute-start.11 = (bf16[40,5760]{1,0:T(8,128)(2,1)S(1)}, bf16[40,5760]{1,0:T(8,128)(2,1)S(1)}, u32[]{:S(2)}, u32[]{:S(2)}) collective-permute-start(bf16[40,5760]{1,0:T(8,128)(2,1)S(1)} %collective-permute-done.9), channel_id=1, source_target_pairs={{0,30},{2,0},{4,2},{6,4},{8,6},{10,8},{12,10},{14,12},{16,14},{18,... | collective-permute-start | bytes 1382408 | tf_op jit(solution)/shard_map/ppermute | solution.py:19
  113.6 12.1 %collective-permute-start.12 = (bf16[40,5760]{1,0:T(8,128)(2,1)S(1)}, bf16[40,5760]{1,0:T(8,128)(2,1)S(1)}, u32[]{:S(2)}, u32[]{:S(2)}) collective-permute-start(bf16[40,5760]{1,0:T(8,128)(2,1)S(1)} %collective-permute-done.10), channel_id=1, source_target_pairs={{0,2},{2,4},{4,6},{6,8},{8,10},{10,12},{12,14},{14,16},{16,18},{18... | collective-permute-start | bytes 1382408 | tf_op jit(solution)/shard_map/ppermute | solution.py:16
  120.0 13.9 %collective-permute-start.13 = (bf16[40,5760]{1,0:T(8,128)(2,1)S(1)}, bf16[40,5760]{1,0:T(8,128)(2,1)S(1)}, u32[]{:S(2)}, u32[]{:S(2)}) collective-permute-start(bf16[40,5760]{1,0:T(8,128)(2,1)S(1)} %collective-permute-done.11), channel_id=1, source_target_pairs={{0,30},{2,0},{4,2},{6,4},{8,6},{10,8},{12,10},{14,12},{16,14},{18,... | collective-permute-start | bytes 1382408 | tf_op jit(solution)/shard_map/ppermute | solution.py:19
  125.6 13.1 %collective-permute-start.14 = (bf16[40,5760]{1,0:T(8,128)(2,1)S(1)}, bf16[40,5760]{1,0:T(8,128)(2,1)S(1)}, u32[]{:S(2)}, u32[]{:S(2)}) collective-permute-start(bf16[40,5760]{1,0:T(8,128)(2,1)S(1)} %collective-permute-done.12), channel_id=1, source_target_pairs={{0,2},{2,4},{4,6},{6,8},{8,10},{10,12},{12,14},{14,16},{16,18},{18... | collective-permute-start | bytes 1382408 | tf_op jit(solution)/shard_map/ppermute | solution.py:16
  156.9 2.5 copy-start.6
  156.9 2.5 copy-start.7
  168.5 4.3 copy-start.8
  168.5 4.3 copy-start.9
  168.5 4.3 copy-start.10
  168.5 4.3 copy-start.11
  182.6 3.2 copy-start.3
  207.6 0.7 copy-start.14
  207.6 0.7 copy-start.15
  208.7 51.9 %collective-permute-start.15 = (bf16[1,80,256]{2,1,0:T(8,128)(2,1)S(1)}, bf16[1,80,256]{2,1,0:T(8,128)(2,1)S(1)}, u32[]{:S(2)}, u32[]{:S(2)}) collective-permute-start(bf16[1,80,256]{2,1,0:T(8,128)(2,1)S(1)} %fusion.5), channel_id=1, source_target_pairs={{2,0},{4,2},{6,4},{8,6},{10,8},{12,10},{14,12},{16,14},{18,16},{20... | collective-permute-start | bytes 122888 | tf_op jit(solution)/shard_map/ppermute | solution.py:34
  210.3 50.7 %collective-permute-start.16 = (bf16[1,80,256]{2,1,0:T(8,128)(2,1)S(1)}, bf16[1,80,256]{2,1,0:T(8,128)(2,1)S(1)}, u32[]{:S(2)}, u32[]{:S(2)}) collective-permute-start(bf16[1,80,256]{2,1,0:T(8,128)(2,1)S(1)} %fusion.6), channel_id=1, source_target_pairs={{0,2},{2,4},{4,6},{6,8},{8,10},{10,12},{12,14},{14,16},{16,18},{18... | collective-permute-start | bytes 122888 | tf_op jit(solution)/shard_map/ppermute | solution.py:33
  259.9 1.8 copy-start.1
Sparse Core Ops, SparseCore 0:
  207.8 261.2 all-reduce.5
